TPU v7x, 128 devices: a whole 4x4x4 slice. The times are simulated.
128 devices in a mesh: gx: 16 (over z, x), gy: 8 (over y, core).
Axes of the slice: x: 4, y: 4, z: 4, core: 2. Of those that a mesh axis runs over, the one named last changes fastest.
Arguments:
- cotangent: float32 [16, 8, 42, 1024], P('gx', 'gy'), may hold values from -6 to 6
- section_states: bfloat16 [3, 16, 8, 42, 1024], P(None, 'gx', 'gy'), may hold values from -6 to 6
- inverse_area: float32 [16, 8, 1024], P('gx', 'gy'), may hold values from 0.5 to 2
- edge_length: float32 [16, 8, 3, 1024], P('gx', 'gy'), may hold values from 0.5 to 1.5
- roughness: float32 [16, 8, 1024], P('gx', 'gy'), may hold values from 0.5 to 2
- soil_conductance: float32 [16, 8, 1024], P('gx', 'gy'), may hold values from 0.5 to 2
- zone_friction: float32 [512], replicated, may hold values from 0.25 to 1
- zone_conductivity: float32 [512], replicated, may hold values from 0.25 to 1
- wet_mask: int32 [16, 8, 1024], P('gx', 'gy'), may hold values 0 or 1
- element_zone: int32 [16, 8, 1024], P('gx', 'gy'), may hold values from 0 to 511, as said below
- send_face: int32 [16, 8, 8, 256], P('gx', 'gy'), may hold values from 0 to 3071, as said below
- send_count: int32 [16, 8, 8], P('gx', 'gy'), may hold values from 0 to 256, as said below
- face_partner: int32 [16, 8, 3, 1024], P('gx', 'gy'), may hold values from 0 to 4867, as said below
- volume_matrix: float32 [12, 12], replicated, may hold values from -1.75 to 1.75
- flux_in: float32 [8, 8], replicated, may hold values from -2 to 2
- flux_out: float32 [8, 8], replicated, may hold values from -2 to 2
Outputs:
- adjoint: float32 [16, 8, 42, 1024], P('gx', 'gy')
- zone_grads: float32 [2, 512], replicated
Inputs may be any that keep to these rules, and one draw needn't show every extreme that they name: `element_zone`: zones lie near their partition: an element of partition (a, b) has a zone among the 8 zones from (a*8+b)*4 on, modulo 512. send_count[a, b, n] equals send_count of the partition at offset n for offset 7 - n; it is 0 where that partition lies outside the grid, 1 to 4 for the four diagonal offsets (4 for some pair in every draw), at least 192 for the others, and 256 for some pair in every draw. `send_face`: the live slots of a partition name distinct faces; slots at or beyond the count hold 0. `face_partner`: the faces are paired: a face sent in slot j to offset n faces entry 3072 + n*256 + j, the other faces face a local face whose partner they are, or themselves.
All inputs are finite; a program needn't handle non-finite values. No bound on the sum of `wet_mask` on one device may be relied on, other than what follows from the above.
Results may differ from a plain program's by a relative error of at most 0.0003.
Values may be sent and summed in bfloat16 or wider, within the bound.
A program may use at most 64 MiB of HBM per device.

v0:
```python
import jax
import jax.numpy as jnp
import numpy as np
from jax import lax
from jax.sharding import PartitionSpec as P

LAYERS = 10
ZONE_DEV = 4
TIME_STEP = 0.2
SALT_RETURN = 0.5
LATERAL = 0.5
GRAD_WEIGHT = 1.0 / 64.0
FACE_NODES = ((1, 2), (2, 0), (0, 1))
MOMENTUM_ROWS = np.array([0, 0, 0, 1, 1, 1, 1, 1, 1, 0, 0, 0], np.float32)


def shifted(x, axis, by):
    peers = lax.axis_size(axis)
    pairs = [(i, i + by) for i in range(peers) if 0 <= i + by < peers]
    return lax.ppermute(x, axis, pairs)


def trace_rows():
    channels = 8 + 2 * LAYERS
    rows = np.zeros((channels, 3), np.int32)
    for face_no in range(3):
        for end_no in range(2):
            node_no = FACE_NODES[face_no][end_no]
            for comp_no in range(4):
                rows[comp_no * 2 + end_no, face_no] = comp_no * 3 + node_no
            for layer_no in range(LAYERS):
                rows[8 + layer_no * 2 + end_no, face_no] = 12 + layer_no * 3 + node_no
    return rows.reshape(-1)


def take_traces(state, rows):
    channels = rows.shape[0] // 3
    return state[rows].reshape(channels, 3 * state.shape[1])


def lift_back(flux, rows, row_count):
    return jnp.zeros((row_count, flux.shape[-1]), jnp.float32).at[rows].add(flux)


def section_speed(flat_traces, outer_flat):
    return jnp.sqrt(1.0 + 0.25 * jnp.mean(flat_traces[:8] ** 2 + outer_flat[:8] ** 2, axis=0))


def local_operator(
    state,
    received,
    conductivity,
    friction,
    wave_speed,
    inverse_area,
    edge_length,
    wet_mask,
    partner,
    volume_matrix,
    flux_in,
    flux_out,
    rows,
):
    element_count = state.shape[1]
    channels = rows.shape[0] // 3
    flat_traces = take_traces(state, rows)
    trace_table = jnp.concatenate([flat_traces, received.reshape(channels, -1)], axis=1)
    outer_traces = trace_table[:, partner.reshape(-1)].reshape(channels, 3, element_count)
    inner_traces = flat_traces.reshape(channels, 3, element_count)
    surf_inner = inner_traces[:8]
    surf_outer = outer_traces[:8]
    flux_surface = (
        jnp.einsum("ab,bfe->afe", flux_in, surf_inner, precision=lax.Precision.HIGHEST)
        - jnp.einsum("ab,bfe->afe", flux_out, surf_outer, precision=lax.Precision.HIGHEST)
        + 0.5 * wave_speed[None] * (surf_inner - surf_outer)
    )
    flux_pore = LATERAL * conductivity[None, None] * (outer_traces[8:] - inner_traces[8:])
    flux_all = jnp.concatenate([flux_surface, flux_pore], axis=0) * edge_length[None]
    lifted = lift_back(flux_all.reshape(channels * 3, element_count), rows, state.shape[0])
    volume = jnp.dot(volume_matrix, state[:12], precision=lax.Precision.HIGHEST)
    top_exchange = conductivity[None] * (state[9:12] - state[12:15])
    momentum = jnp.asarray(MOMENTUM_ROWS, dtype=jnp.float32)[:, None]
    surface = inverse_area[None] * (volume + lifted[:12]) - momentum * friction[None] * state[:12]
    surface = (
        jnp.concatenate([surface[:9], surface[9:12] - SALT_RETURN * top_exchange], axis=0)
        * wet_mask[None]
    )
    layers = state[12:].reshape(LAYERS, 3, element_count)
    between = conductivity[None, None] * (layers[:-1] - layers[1:])
    from_above = jnp.concatenate([top_exchange[None], between], axis=0)
    to_below = jnp.concatenate([between, jnp.zeros((1, 3, element_count), jnp.float32)], axis=0)
    pore = (from_above - to_below).reshape(3 * LAYERS, element_count) + inverse_area[None] * lifted[
        12:
    ]
    return jnp.concatenate([surface, pore], axis=0)


def forward_estuary(block, by_count):
    return shifted(block, "gx", by_count)


def forward_across(block, by_count):
    return shifted(block, "gy", by_count)


def backward_estuary(block, by_count):
    return shifted(block, "gx", by_count)


def backward_across(block, by_count):
    return shifted(block, "gy", by_count)


def route_blocks(blocks, estuary_hop, across_hop):
    pieces = [
        across_hop(estuary_hop(blocks[..., 7, :], 1), 1),
        estuary_hop(blocks[..., 6, :], 1),
        across_hop(estuary_hop(blocks[..., 5, :], 1), -1),
        across_hop(blocks[..., 4, :], 1),
        across_hop(blocks[..., 3, :], -1),
        across_hop(estuary_hop(blocks[..., 2, :], -1), 1),
        estuary_hop(blocks[..., 1, :], -1),
        across_hop(estuary_hop(blocks[..., 0, :], -1), -1),
    ]
    return jnp.stack(pieces, axis=-2)


def local(
    cotangent,
    section_states,
    inverse_area,
    edge_length,
    roughness,
    soil_conductance,
    zone_friction,
    zone_conductivity,
    wet_mask,
    element_zone,
    send_face,
    send_count,
    face_partner,
    volume_matrix,
    flux_in,
    flux_out,
):
    rows = jnp.asarray(trace_rows(), dtype=jnp.int32)
    channels = rows.shape[0] // 3
    cotangent_local = cotangent[0, 0]
    row_count = cotangent_local.shape[0]
    element_count = cotangent_local.shape[1]
    area_local = inverse_area[0, 0]
    edges_local = edge_length[0, 0]
    rough_local = roughness[0, 0]
    conduct_local = soil_conductance[0, 0]
    wetness = wet_mask[0, 0].astype(jnp.float32)
    zones_local = element_zone[0, 0]
    faces_sent = send_face[0, 0]
    counts_sent = send_count[0, 0]
    partner = face_partner[0, 0]
    zone_total = zone_friction.shape[0]
    conductivity = zone_conductivity[zones_local] * conduct_local
    zone_factor = zone_friction[zones_local]
    slot_index = jnp.arange(faces_sent.shape[1])
    live_slots = (slot_index[None, :] < counts_sent[:, None]).astype(jnp.float32)
    device_number = lax.axis_index("gx") * lax.axis_size("gy") + lax.axis_index("gy")
    zone_base = device_number * ZONE_DEV
    near_count = 2 * ZONE_DEV
    offset_zone = (zones_local - zone_base) % zone_total
    near_onehot = (offset_zone[None, :] == jnp.arange(near_count, dtype=jnp.int32)[:, None]).astype(
        jnp.float32
    )
    near_ids = (zone_base + jnp.arange(near_count, dtype=jnp.int32)) % zone_total
    forward_all = section_states[:, 0, 0].astype(jnp.float32)

    def section_received(states):
        flat_states = jax.vmap(lambda one: take_traces(one, rows))(states)
        outgoing = (flat_states[:, :, faces_sent] * live_slots[None, None]).astype(jnp.bfloat16)
        return route_blocks(outgoing, forward_estuary, forward_across).astype(jnp.float32)

    def received_of(section_no):
        return section_received(forward_all[section_no : section_no + 1])[0]

    def section_adjoint(section_no, weight_field):
        forward_state = forward_all[section_no]
        flat_forward = take_traces(forward_state, rows)
        received = received_of(section_no)
        trace_table = jnp.concatenate([flat_forward, received.reshape(channels, -1)], axis=1)
        outer_forward = trace_table[:, partner.reshape(-1)]
        wave_speed = section_speed(flat_forward, outer_forward).reshape(3, element_count)
        moment = jnp.sqrt(1.0 + jnp.mean(forward_state[3:9] ** 2, axis=0))
        friction_base = rough_local * moment
        friction = zone_factor * friction_base

        def section_operator(state, incoming, conduct_in, friction_in):
            return local_operator(
                state,
                incoming,
                conduct_in,
                friction_in,
                wave_speed,
                area_local,
                edges_local,
                wetness,
                partner,
                volume_matrix,
                flux_in,
                flux_out,
                rows,
            )

        unused, pullback = jax.vjp(
            section_operator, forward_state, received, conductivity, friction
        )
        state_bar, received_bar, conduct_bar, friction_bar = pullback(TIME_STEP * weight_field)
        returned = route_blocks(received_bar, backward_estuary, backward_across)
        flat_bar = (
            jnp.zeros((channels, 3 * element_count), jnp.float32)
            .at[:, faces_sent]
            .add(returned * live_slots[None])
        )
        state_bar = state_bar + lift_back(
            flat_bar.reshape(channels * 3, element_count), rows, row_count
        )
        element_terms = jnp.stack(
            [friction_base * friction_bar, conduct_local * conduct_bar], axis=0
        )
        near_terms = jnp.einsum(
            "ke,ze->kz", element_terms, near_onehot, precision=lax.Precision.HIGHEST
        )
        zone_terms = jnp.zeros((2, zone_total), jnp.float32).at[:, near_ids].add(near_terms)
        return (state_bar, zone_terms)

    bar_two, terms_two = section_adjoint(2, cotangent_local)
    lam_two = 2.0 / 3.0 * (cotangent_local + bar_two)
    bar_one, terms_one = section_adjoint(1, lam_two)
    lam_one = 0.25 * (lam_two + bar_one)
    bar_zero, terms_zero = section_adjoint(0, lam_one)
    adjoint = cotangent_local / 3.0 + 0.75 * lam_two + lam_one + bar_zero
    summed = [lax.psum(terms, ("gx", "gy")) for terms in (terms_two, terms_one, terms_zero)]
    zone_grads = GRAD_WEIGHT * (2.0 / 3.0 * summed[0] + 0.25 * summed[1] + summed[2])
    return (adjoint[None, None], zone_grads)


def solution(mesh):
    placed = (
        P("gx", "gy", None, None),
        P(None, "gx", "gy", None, None),
        P("gx", "gy", None),
        P("gx", "gy", None, None),
        P("gx", "gy", None),
        P("gx", "gy", None),
        P(),
        P(),
        P("gx", "gy", None),
        P("gx", "gy", None),
        P("gx", "gy", None, None),
        P("gx", "gy", None),
        P("gx", "gy", None, None),
        P(),
        P(),
        P(),
    )
    return jax.shard_map(
        local,
        mesh=mesh,
        in_specs=placed,
        out_specs=(P("gx", "gy", None, None), P()),
        check_vma=False,
    )
```

profile of v0, /device:TPU:41, one launch (start us, length us, event | category | flops | bytes accessed | tf_op | source)
XLA Modules:
  0.0 641.6 jit_solution(15260128408146421137)
XLA Ops:
  5.4 7.6 %gather_fusion.12 = f32[2048,28]{1,0:T(8,128)} fusion(f32[28,3072]{0,1:T(8,128)S(1)} %copy.369, s32[2048]{0:T(1024)S(1)} %broadcast_clamp_fusion.1), kind=kCustom, calls=%fused_computation.15 | custom fusion | bytes 466944 | tf_op jit(solution)/shard_map/gather | solution.py:177
  17.5 7.6 %gather_fusion.8 = f32[2048,28]{1,0:T(8,128)} fusion(f32[28,3072]{0,1:T(8,128)S(1)} %copy.340, s32[2048]{0:T(1024)S(1)} %broadcast_clamp_fusion.1), kind=kCustom, calls=%fused_computation.10 | custom fusion | bytes 466944 | tf_op jit(solution)/shard_map/gather | solution.py:177
  29.0 7.6 %gather_fusion.4 = f32[2048,28]{1,0:T(8,128)} fusion(f32[28,3072]{0,1:T(8,128)S(1)} %copy.311, s32[2048]{0:T(1024)S(1)} %broadcast_clamp_fusion.1), kind=kCustom, calls=%fused_computation.5 | custom fusion | bytes 466944 | tf_op jit(solution)/shard_map/gather | solution.py:177
  49.9 4.6 collective-permute-start.5
  59.3 6.9 %gather_fusion = f32[1024]{0:T(1024)S(1)} fusion(f32[512]{0:T(512)S(1)} %copy-done.1, s32[1024]{0:T(1024)S(1)} %broadcast_clamp_fusion.2), kind=kCustom, calls=%fused_computation | custom fusion | bytes 12288 | tf_op jit(solution)/shard_map/gather | solution.py:161
  66.2 6.9 %gather_fusion.1 = f32[1024]{0:T(1024)S(1)} fusion(f32[512]{0:T(512)S(1)} %copy-done.2, s32[1024]{0:T(1024)S(1)} %broadcast_clamp_fusion.2), kind=kCustom, calls=%fused_computation.1 | custom fusion | bytes 12288 | tf_op jit(solution)/shard_map/gather | solution.py:162
  82.1 4.6 collective-permute-start.7
  94.7 4.8 collective-permute-start.29
  113.6 5.8 collective-permute-start.57
  150.4 5.5 collective-permute-start.31
  162.7 4.5 collective-permute-start.25
  172.6 10.9 %gather_fusion.5 = f32[3072,28]{1,0:T(8,128)} fusion(f32[28,5120]{0,1:T(8,128)S(1)} %copy.321, s32[3072]{0:T(1024)S(1)} %copy-done.60), kind=kCustom, calls=%fused_computation.6 | custom fusion | bytes 700416 | tf_op jit(solution)/shard_map/gather | solution.py:188
  190.1 17.9 %scatter_custom_fusion = f32[28,5120]{0,1:T(8,128)S(1)} fusion(s32[3072]{0:T(1024)} %bitcast.397, f32[3072,28]{1,0:T(8,128)} %copy.327, f32[]{:T(128)} %constant.38.clone.1), kind=kCustom, calls=%fused_computation.36 | custom fusion | flops 86016 | bytes 573952 | tf_op jit(solution)/shard_map/transpose(jvp())/scatter-add | solution.py:68
  211.8 5.5 collective-permute-start.55
  249.4 11.9 %gather_fusion.9 = f32[3072,28]{1,0:T(8,128)} fusion(f32[28,5120]{0,1:T(8,128)S(1)} %copy.350, s32[3072]{0:T(1024)} %broadcast_clamp_fusion), kind=kCustom, calls=%fused_computation.11 | custom fusion | bytes 700416 | tf_op jit(solution)/shard_map/gather | solution.py:188
  273.2 4.5 collective-permute-start.17
  284.4 11.9 %gather_fusion.13 = f32[3072,28]{1,0:T(8,128)} fusion(f32[28,5120]{0,1:T(8,128)S(1)} %copy.379, s32[3072]{0:T(1024)} %broadcast_clamp_fusion), kind=kCustom, calls=%fused_computation.16 | custom fusion | bytes 700416 | tf_op jit(solution)/shard_map/gather | solution.py:188
  336.6 13.9 %scatter_custom_fusion.2 = f32[28,3072]{0,1:T(8,128)S(1)} fusion(s32[2048]{0:T(1024)} %bitcast.407, f32[2048,28]{1,0:T(8,128)} %bitcast.370, f32[]{:T(128)} %constant.38.clone.1), kind=kCustom, calls=%fused_computation.57 | custom fusion | flops 57344 | bytes 344576 | tf_op jit(solution)/shard_map/scatter-add | solution.py:219
  363.1 17.9 %scatter_custom_fusion.4 = f32[28,5120]{0,1:T(8,128)S(1)} fusion(s32[3072]{0:T(1024)} %bitcast.398, f32[3072,28]{1,0:T(8,128)} %copy.356, f32[]{:T(128)} %constant.38.clone.1), kind=kCustom, calls=%fused_computation.34 | custom fusion | flops 86016 | bytes 573952 | tf_op jit(solution)/shard_map/transpose(jvp())/scatter-add | solution.py:68
  424.2 4.5 collective-permute-start.37
  448.8 13.6 %scatter_custom_fusion.6 = f32[28,3072]{0,1:T(8,128)S(1)} fusion(s32[2048]{0:T(1024)} %bitcast.408, f32[2048,28]{1,0:T(8,128)S(1)} %bitcast.371, f32[]{:T(128)} %constant.38.clone.1), kind=kCustom, calls=%fused_computation.55 | custom fusion | flops 57344 | bytes 344576 | tf_op jit(solution)/shard_map/scatter-add | solution.py:219
  474.9 17.9 %scatter_custom_fusion.8 = f32[28,5120]{0,1:T(8,128)S(1)} fusion(s32[3072]{0:T(1024)} %bitcast.399, f32[3072,28]{1,0:T(8,128)} %copy.385, f32[]{:T(128)} %constant.38.clone.1), kind=kCustom, calls=%fused_computation.32 | custom fusion | flops 86016 | bytes 573952 | tf_op jit(solution)/shard_map/transpose(jvp())/scatter-add | solution.py:68
  518.1 69.9 %all-reduce.42 = (f32[2,512]{0,1:T(8,128)}, f32[2,512]{0,1:T(8,128)}, f32[2,512]{0,1:T(8,128)}) all-reduce(f32[2,512]{0,1:T(8,128)S(1)} %scatter_custom_fusion.14, f32[2,512]{0,1:T(8,128)S(1)} %scatter_custom_fusion.13, f32[2,512]{0,1:T(8,128)} %scatter_custom_fusion.12), channel_id=1, replica_groups=mesh['gx'=16,'gy'=8] {'gx','gy'}, use_global_device_ids=true, to_apply=%region_35.36 | all-reduce | flops 3072 | bytes 24576 | tf_op jit(solution)/shard_map/psum | solution.py:239
  624.9 13.6 %scatter_custom_fusion.10 = f32[28,3072]{0,1:T(8,128)S(1)} fusion(s32[2048]{0:T(1024)} %bitcast.409, f32[2048,28]{1,0:T(8,128)S(1)} %bitcast.369, f32[]{:T(128)} %constant.38.clone.1), kind=kCustom, calls=%fused_computation.53 | custom fusion | flops 57344 | bytes 344576 | tf_op jit(solution)/shard_map/scatter-add | solution.py:219
  (732 shorter events, 356.8 us)
Async XLA Ops:
  40.8 41.3 %collective-permute-start = (bf16[1,28,256]{2,1,0:T(8,128)(2,1)}, bf16[1,28,256]{2,1,0:T(8,128)(2,1)}, u32[]{:S(2)}, u32[]{:S(2)}) collective-permute-start(bf16[1,28,256]{2,1,0:T(8,128)(2,1)} %get-tuple-element.115), channel_id=1, source_target_pairs={{0,8},{8,16},{16,24},{24,32},{32,40},{40,48},{48,56},{56,64},{64,7... | collective-permute-start | bytes 43016 | tf_op jit(solution)/shard_map/ppermute | solution.py:20
  43.9 42.7 %collective-permute-start.2 = (bf16[1,28,256]{2,1,0:T(8,128)(2,1)}, bf16[1,28,256]{2,1,0:T(8,128)(2,1)}, u32[]{:S(2)}, u32[]{:S(2)}) collective-permute-start(bf16[1,28,256]{2,1,0:T(8,128)(2,1)} %get-tuple-element.114), channel_id=1, source_target_pairs={{0,8},{8,16},{16,24},{24,32},{32,40},{40,48},{48,56},{56,64},{64,7... | collective-permute-start | bytes 43016 | tf_op jit(solution)/shard_map/ppermute | solution.py:20
  47.0 42.4 %collective-permute-start.3 = (bf16[1,28,256]{2,1,0:T(8,128)(2,1)}, bf16[1,28,256]{2,1,0:T(8,128)(2,1)}, u32[]{:S(2)}, u32[]{:S(2)}) collective-permute-start(bf16[1,28,256]{2,1,0:T(8,128)(2,1)} %get-tuple-element.113), channel_id=1, source_target_pairs={{0,8},{8,16},{16,24},{24,32},{32,40},{40,48},{48,56},{56,64},{64,7... | collective-permute-start | bytes 43016 | tf_op jit(solution)/shard_map/ppermute | solution.py:20
  49.9 41.7 %collective-permute-start.5 = (bf16[1,28,256]{2,1,0:T(8,128)(2,1)}, bf16[1,28,256]{2,1,0:T(8,128)(2,1)}, u32[]{:S(2)}, u32[]{:S(2)}) collective-permute-start(bf16[1,28,256]{2,1,0:T(8,128)(2,1)} %get-tuple-element.112), channel_id=1, source_target_pairs={{0,1},{1,2},{2,3},{3,4},{4,5},{5,6},{6,7},{8,9},{9,10},{10,11},{11... | collective-permute-start | bytes 43016 | tf_op jit(solution)/shard_map/ppermute | solution.py:20
  54.5 40.3 %collective-permute-start.6 = (bf16[1,28,256]{2,1,0:T(8,128)(2,1)}, bf16[1,28,256]{2,1,0:T(8,128)(2,1)}, u32[]{:S(2)}, u32[]{:S(2)}) collective-permute-start(bf16[1,28,256]{2,1,0:T(8,128)(2,1)} %get-tuple-element.111), channel_id=1, source_target_pairs={{1,0},{2,1},{3,2},{4,3},{5,4},{6,5},{7,6},{9,8},{10,9},{11,10},{12... | collective-permute-start | bytes 43016 | tf_op jit(solution)/shard_map/ppermute | solution.py:20
  124.0 36.8 %collective-permute-start.24 = (bf16[1,28,256]{2,1,0:T(8,128)(2,1)S(1)}, bf16[1,28,256]{2,1,0:T(8,128)(2,1)}, u32[]{:S(2)}, u32[]{:S(2)}) collective-permute-start(bf16[1,28,256]{2,1,0:T(8,128)(2,1)S(1)} %get-tuple-element.107), channel_id=1, source_target_pairs={{0,8},{8,16},{16,24},{24,32},{32,40},{40,48},{48,56},{56,64},{64,7... | collective-permute-start | bytes 43016 | tf_op jit(solution)/shard_map/ppermute | solution.py:20
  125.9 36.8 %collective-permute-start.27 = (bf16[1,28,256]{2,1,0:T(8,128)(2,1)S(1)}, bf16[1,28,256]{2,1,0:T(8,128)(2,1)}, u32[]{:S(2)}, u32[]{:S(2)}) collective-permute-start(bf16[1,28,256]{2,1,0:T(8,128)(2,1)S(1)} %get-tuple-element.105), channel_id=1, source_target_pairs={{0,8},{8,16},{16,24},{24,32},{32,40},{40,48},{48,56},{56,64},{64,7... | collective-permute-start | bytes 43016 | tf_op jit(solution)/shard_map/ppermute | solution.py:20
  150.4 59.4 %collective-permute-start.31 = (bf16[1,28,256]{2,1,0:T(8,128)(2,1)}, bf16[1,28,256]{2,1,0:T(8,128)(2,1)}, u32[]{:S(2)}, u32[]{:S(2)}) collective-permute-start(bf16[1,28,256]{2,1,0:T(8,128)(2,1)} %get-tuple-element.102), channel_id=1, source_target_pairs={{8,0},{16,8},{24,16},{32,24},{40,32},{48,40},{56,48},{64,56},{72,6... | collective-permute-start | bytes 43016 | tf_op jit(solution)/shard_map/ppermute | solution.py:20
  156.6 55.2 %collective-permute-start.34 = (bf16[1,28,256]{2,1,0:T(8,128)(2,1)}, bf16[1,28,256]{2,1,0:T(8,128)(2,1)}, u32[]{:S(2)}, u32[]{:S(2)}) collective-permute-start(bf16[1,28,256]{2,1,0:T(8,128)(2,1)} %get-tuple-element.100), channel_id=1, source_target_pairs={{8,0},{16,8},{24,16},{32,24},{40,32},{48,40},{56,48},{64,56},{72,6... | collective-permute-start | bytes 43016 | tf_op jit(solution)/shard_map/ppermute | solution.py:20
  160.8 56.6 %collective-permute-start.48 = (bf16[1,28,256]{2,1,0:T(8,128)(2,1)}, bf16[1,28,256]{2,1,0:T(8,128)(2,1)}, u32[]{:S(2)}, u32[]{:S(2)}) collective-permute-start(bf16[1,28,256]{2,1,0:T(8,128)(2,1)} %get-tuple-element.99), channel_id=1, source_target_pairs={{0,8},{8,16},{16,24},{24,32},{32,40},{40,48},{48,56},{56,64},{64,7... | collective-permute-start | bytes 43016 | tf_op jit(solution)/shard_map/ppermute | solution.py:20
  162.7 58.0 %collective-permute-start.25 = (bf16[1,28,256]{2,1,0:T(8,128)(2,1)}, bf16[1,28,256]{2,1,0:T(8,128)(2,1)}, u32[]{:S(2)}, u32[]{:S(2)}) collective-permute-start(bf16[1,28,256]{2,1,0:T(8,128)(2,1)} %collective-permute-done.24), channel_id=1, source_target_pairs={{0,1},{1,2},{2,3},{3,4},{4,5},{5,6},{6,7},{8,9},{9,10},{10,11},{11... | collective-permute-start | bytes 43016 | tf_op jit(solution)/shard_map/ppermute | solution.py:20
  167.2 58.0 %collective-permute-start.28 = (bf16[1,28,256]{2,1,0:T(8,128)(2,1)}, bf16[1,28,256]{2,1,0:T(8,128)(2,1)}, u32[]{:S(2)}, u32[]{:S(2)}) collective-permute-start(bf16[1,28,256]{2,1,0:T(8,128)(2,1)} %collective-permute-done.27), channel_id=1, source_target_pairs={{1,0},{2,1},{3,2},{4,3},{5,4},{6,5},{7,6},{9,8},{10,9},{11,10},{12... | collective-permute-start | bytes 43016 | tf_op jit(solution)/shard_map/ppermute | solution.py:20
  237.7 35.4 %collective-permute-start.56 = (bf16[1,28,256]{2,1,0:T(8,128)(2,1)}, bf16[1,28,256]{2,1,0:T(8,128)(2,1)}, u32[]{:S(2)}, u32[]{:S(2)}) collective-permute-start(bf16[1,28,256]{2,1,0:T(8,128)(2,1)} %collective-permute-done.55), channel_id=1, source_target_pairs={{0,1},{1,2},{2,3},{3,4},{4,5},{5,6},{6,7},{8,9},{9,10},{10,11},{11... | collective-permute-start | bytes 43016 | tf_op jit(solution)/shard_map/ppermute | solution.py:20
  241.4 37.0 %collective-permute-start.59 = (bf16[1,28,256]{2,1,0:T(8,128)(2,1)}, bf16[1,28,256]{2,1,0:T(8,128)(2,1)}, u32[]{:S(2)}, u32[]{:S(2)}) collective-permute-start(bf16[1,28,256]{2,1,0:T(8,128)(2,1)} %collective-permute-done.58), channel_id=1, source_target_pairs={{1,0},{2,1},{3,2},{4,3},{5,4},{6,5},{7,6},{9,8},{10,9},{11,10},{12... | collective-permute-start | bytes 43016 | tf_op jit(solution)/shard_map/ppermute | solution.py:20
  243.4 55.2 %collective-permute-start.12 = (f32[28,256]{1,0:T(8,128)}, f32[28,256]{1,0:T(8,128)}, u32[]{:S(2)}, u32[]{:S(2)}) collective-permute-start(f32[28,256]{1,0:T(8,128)} %bitcast.43), channel_id=1, source_target_pairs={{0,8},{8,16},{16,24},{24,32},{32,40},{40,48},{48,56},{56,64},{64,7... | collective-permute-start | bytes 86024 | tf_op jit(solution)/shard_map/ppermute | solution.py:20
  266.8 35.9 %collective-permute-start.14 = (f32[28,256]{1,0:T(8,128)}, f32[28,256]{1,0:T(8,128)}, u32[]{:S(2)}, u32[]{:S(2)}) collective-permute-start(f32[28,256]{1,0:T(8,128)} %bitcast.44), channel_id=1, source_target_pairs={{0,8},{8,16},{16,24},{24,32},{32,40},{40,48},{48,56},{56,64},{64,7... | collective-permute-start | bytes 86024 | tf_op jit(solution)/shard_map/ppermute | solution.py:20
  269.5 37.7 %collective-permute-start.15 = (f32[28,256]{1,0:T(8,128)}, f32[28,256]{1,0:T(8,128)}, u32[]{:S(2)}, u32[]{:S(2)}) collective-permute-start(f32[28,256]{1,0:T(8,128)} %bitcast.45), channel_id=1, source_target_pairs={{0,8},{8,16},{16,24},{24,32},{32,40},{40,48},{48,56},{56,64},{64,7... | collective-permute-start | bytes 86024 | tf_op jit(solution)/shard_map/ppermute | solution.py:20
  273.2 37.3 %collective-permute-start.17 = (f32[28,256]{1,0:T(8,128)}, f32[28,256]{1,0:T(8,128)}, u32[]{:S(2)}, u32[]{:S(2)}) collective-permute-start(f32[28,256]{1,0:T(8,128)} %bitcast.46), channel_id=1, source_target_pairs={{0,1},{1,2},{2,3},{3,4},{4,5},{5,6},{6,7},{8,9},{9,10},{10,11},{11... | collective-permute-start | bytes 86024 | tf_op jit(solution)/shard_map/ppermute | solution.py:20
  278.4 36.6 %collective-permute-start.18 = (f32[28,256]{1,0:T(8,128)}, f32[28,256]{1,0:T(8,128)}, u32[]{:S(2)}, u32[]{:S(2)}) collective-permute-start(f32[28,256]{1,0:T(8,128)} %bitcast.47), channel_id=1, source_target_pairs={{1,0},{2,1},{3,2},{4,3},{5,4},{6,5},{7,6},{9,8},{10,9},{11,10},{12... | collective-permute-start | bytes 86024 | tf_op jit(solution)/shard_map/ppermute | solution.py:20
  495.6 97.7 %collective-permute-start.60 = (f32[28,256]{1,0:T(8,128)}, f32[28,256]{1,0:T(8,128)}, u32[]{:S(2)}, u32[]{:S(2)}) collective-permute-start(f32[28,256]{1,0:T(8,128)} %bitcast.119), channel_id=1, source_target_pairs={{0,8},{8,16},{16,24},{24,32},{32,40},{40,48},{48,56},{56,64},{64,7... | collective-permute-start | bytes 86024 | tf_op jit(solution)/shard_map/ppermute | solution.py:20
  499.2 98.4 %collective-permute-start.62 = (f32[28,256]{1,0:T(8,128)}, f32[28,256]{1,0:T(8,128)}, u32[]{:S(2)}, u32[]{:S(2)}) collective-permute-start(f32[28,256]{1,0:T(8,128)} %bitcast.120), channel_id=1, source_target_pairs={{0,8},{8,16},{16,24},{24,32},{32,40},{40,48},{48,56},{56,64},{64,7... | collective-permute-start | bytes 86024 | tf_op jit(solution)/shard_map/ppermute | solution.py:20
  502.7 99.3 %collective-permute-start.63 = (f32[28,256]{1,0:T(8,128)}, f32[28,256]{1,0:T(8,128)}, u32[]{:S(2)}, u32[]{:S(2)}) collective-permute-start(f32[28,256]{1,0:T(8,128)} %bitcast.121), channel_id=1, source_target_pairs={{0,8},{8,16},{16,24},{24,32},{32,40},{40,48},{48,56},{56,64},{64,7... | collective-permute-start | bytes 86024 | tf_op jit(solution)/shard_map/ppermute | solution.py:20
  506.3 98.4 %collective-permute-start.65 = (f32[28,256]{1,0:T(8,128)}, f32[28,256]{1,0:T(8,128)}, u32[]{:S(2)}, u32[]{:S(2)}) collective-permute-start(f32[28,256]{1,0:T(8,128)} %bitcast.122), channel_id=1, source_target_pairs={{0,1},{1,2},{2,3},{3,4},{4,5},{5,6},{6,7},{8,9},{9,10},{10,11},{11... | collective-permute-start | bytes 86024 | tf_op jit(solution)/shard_map/ppermute | solution.py:20
  510.8 97.0 %collective-permute-start.66 = (f32[28,256]{1,0:T(8,128)S(1)}, f32[28,256]{1,0:T(8,128)}, u32[]{:S(2)}, u32[]{:S(2)}) collective-permute-start(f32[28,256]{1,0:T(8,128)S(1)} %bitcast.402), channel_id=1, source_target_pairs={{1,0},{2,1},{3,2},{4,3},{5,4},{6,5},{7,6},{9,8},{10,9},{11,10},{12... | collective-permute-start | bytes 86024 | tf_op jit(solution)/shard_map/ppermute | solution.py:20
  (201 other events, 3057.6 us)
where the time goes:
time: 654 us; the launch traced here: 642 us
  starting transfers between devices  219 us (33%)
  local copies, waits for them, and re-layouts  197 us (30%)
  other arithmetic  143 us (22%)
  blocking collectives  69.9 us (11%)
  matrix products  7.69 us (1%)
    ppermute x72, starting transfers between devices, shifted(): return lax.ppermute(x, axis, pairs)  219 us
    psum x1, blocking collectives, local(): lax.psum(terms, ('gx', 'gy'))  69.9 us
    scatter-add x3, other arithmetic, local_operator(): trace_table[:, partner.reshape(-1)].reshape(channels, 3, element_count)  53.6 us
    scatter-add x3, other arithmetic, section_adjoint(): flat_bar = jnp.zeros((channels, 3 * element_count), jnp.float32).at[:, fa...  41.2 us
    gather x6, local copies, waits for them, and re-layouts, section_adjoint(): outer_forward = trace_table[:, partner.reshape(-1)]  40.6 us
    unnamed x343, local copies, waits for them, and re-layouts  36.6 us
    gather x6, local copies, waits for them, and re-layouts, section_received(): flat_states[:, :, faces_sent] * live_slots[None, None]  29 us
    another operation x54, local copies, waits for them, and re-layouts, route_blocks(): return jnp.stack(pieces, axis=-2)  28.7 us
  transfers between devices with their start and end apart: 72, of which 0 were waited for; matrix products, arithmetic and copies ran while one was open for 29% of the time, Pallas kernels for 0%

commit v1 on v0

--- a/solution.py
+++ b/solution.py
@@ -236,7 +236,10 @@
     lam_one = 0.25 * (lam_two + bar_one)
     bar_zero, terms_zero = section_adjoint(0, lam_one)
     adjoint = cotangent_local / 3.0 + 0.75 * lam_two + lam_one + bar_zero
-    summed = [lax.psum(terms, ("gx", "gy")) for terms in (terms_two, terms_one, terms_zero)]
+    summed = [
+        jnp.sum(lax.all_gather(terms, ("gx", "gy")), axis=0)
+        for terms in (terms_two, terms_one, terms_zero)
+    ]
     zone_grads = GRAD_WEIGHT * (2.0 / 3.0 * summed[0] + 0.25 * summed[1] + summed[2])
     return (adjoint[None, None], zone_grads)
 

time: 654 us -> 692 us (1.058)
  blocking collectives: 69.9 us -> 104 us
    all_gather x0 -> x3, blocking collectives: none -> 104 us  [local(): lax.all_gather(terms, ('gx', 'gy'))]
    psum x1 -> x0, blocking collectives: 69.9 us -> none  [local(): lax.psum(terms, ('gx', 'gy'))]
    unnamed x343 -> x351, local copies, waits for them, and re-layouts: 36.6 us -> 38.8 us
  transfers between devices with their start and end apart: 72 -> 72, of which waited for: 0 -> 0; matrix products, arithmetic and copies ran while one was open for 29% -> 28% of each run, Pallas kernels for 0% -> 0%
where the time goes in v1:
time: 692 us; the launch traced here: 678 us
  starting transfers between devices  219 us (32%)
  local copies, waits for them, and re-layouts  199 us (29%)
  other arithmetic  143 us (21%)
  blocking collectives  104 us (15%)
  matrix products  7.66 us (1%)
    ppermute x72, starting transfers between devices, shifted(): return lax.ppermute(x, axis, pairs)  219 us
    all_gather x3, blocking collectives, local(): lax.all_gather(terms, ('gx', 'gy'))  104 us
    scatter-add x3, other arithmetic, local_operator(): trace_table[:, partner.reshape(-1)].reshape(channels, 3, element_count)  53.6 us
    scatter-add x3, other arithmetic, section_adjoint(): flat_bar = jnp.zeros((channels, 3 * element_count), jnp.float32).at[:, fa...  41.2 us
    gather x6, local copies, waits for them, and re-layouts, section_adjoint(): outer_forward = trace_table[:, partner.reshape(-1)]  40.7 us
    unnamed x351, local copies, waits for them, and re-layouts  38.8 us
    gather x6, local copies, waits for them, and re-layouts, section_received(): flat_states[:, :, faces_sent] * live_slots[None, None]  28.9 us
    another operation x54, local copies, waits for them, and re-layouts, route_blocks(): return jnp.stack(pieces, axis=-2)  28.8 us
  transfers between devices with their start and end apart: 72, of which 0 were waited for; matrix products, arithmetic and copies ran while one was open for 28% of the time, Pallas kernels for 0%

profile of v1, /device:TPU:41, one launch (start us, length us, event | category | flops | bytes accessed | tf_op | source)
XLA Modules:
  0.0 678.2 jit_solution(1205340170468812021)
XLA Ops:
  5.4 7.6 %gather_fusion.12 = f32[2048,28]{1,0:T(8,128)} fusion(f32[28,3072]{0,1:T(8,128)S(1)} %copy.379, s32[2048]{0:T(1024)S(1)} %broadcast_clamp_fusion.1), kind=kCustom, calls=%fused_computation.15 | custom fusion | bytes 466944 | tf_op jit(solution)/shard_map/gather | solution.py:177
  17.5 7.6 %gather_fusion.8 = f32[2048,28]{1,0:T(8,128)} fusion(f32[28,3072]{0,1:T(8,128)S(1)} %copy.350, s32[2048]{0:T(1024)S(1)} %broadcast_clamp_fusion.1), kind=kCustom, calls=%fused_computation.10 | custom fusion | bytes 466944 | tf_op jit(solution)/shard_map/gather | solution.py:177
  29.0 7.6 %gather_fusion.4 = f32[2048,28]{1,0:T(8,128)} fusion(f32[28,3072]{0,1:T(8,128)S(1)} %copy.321, s32[2048]{0:T(1024)S(1)} %broadcast_clamp_fusion.1), kind=kCustom, calls=%fused_computation.5 | custom fusion | bytes 466944 | tf_op jit(solution)/shard_map/gather | solution.py:177
  49.9 4.6 collective-permute-start.5
  59.3 6.9 %gather_fusion = f32[1024]{0:T(1024)S(1)} fusion(f32[512]{0:T(512)S(1)} %copy-done.1, s32[1024]{0:T(1024)S(1)} %broadcast_clamp_fusion.2), kind=kCustom, calls=%fused_computation | custom fusion | bytes 12288 | tf_op jit(solution)/shard_map/gather | solution.py:161
  66.2 6.9 %gather_fusion.1 = f32[1024]{0:T(1024)S(1)} fusion(f32[512]{0:T(512)S(1)} %copy-done.2, s32[1024]{0:T(1024)S(1)} %broadcast_clamp_fusion.2), kind=kCustom, calls=%fused_computation.1 | custom fusion | bytes 12288 | tf_op jit(solution)/shard_map/gather | solution.py:162
  82.1 4.6 collective-permute-start.7
  94.8 4.8 collective-permute-start.29
  113.7 5.8 collective-permute-start.57
  150.4 5.5 collective-permute-start.31
  162.7 4.5 collective-permute-start.25
  172.6 10.9 %gather_fusion.5 = f32[3072,28]{1,0:T(8,128)} fusion(f32[28,5120]{0,1:T(8,128)S(1)} %copy.331, s32[3072]{0:T(1024)S(1)} %copy-done.60), kind=kCustom, calls=%fused_computation.6 | custom fusion | bytes 700416 | tf_op jit(solution)/shard_map/gather | solution.py:188
  190.1 17.9 %scatter_custom_fusion = f32[28,5120]{0,1:T(8,128)S(1)} fusion(s32[3072]{0:T(1024)} %bitcast.403, f32[3072,28]{1,0:T(8,128)} %copy.337, f32[]{:T(128)} %constant.38.clone.1), kind=kCustom, calls=%fused_computation.36 | custom fusion | flops 86016 | bytes 573952 | tf_op jit(solution)/shard_map/transpose(jvp())/scatter-add | solution.py:68
  211.9 5.5 collective-permute-start.55
  249.4 11.9 %gather_fusion.9 = f32[3072,28]{1,0:T(8,128)} fusion(f32[28,5120]{0,1:T(8,128)S(1)} %copy.360, s32[3072]{0:T(1024)} %broadcast_clamp_fusion), kind=kCustom, calls=%fused_computation.11 | custom fusion | bytes 700416 | tf_op jit(solution)/shard_map/gather | solution.py:188
  284.5 11.9 %gather_fusion.13 = f32[3072,28]{1,0:T(8,128)} fusion(f32[28,5120]{0,1:T(8,128)S(1)} %copy.389, s32[3072]{0:T(1024)} %broadcast_clamp_fusion), kind=kCustom, calls=%fused_computation.16 | custom fusion | bytes 700416 | tf_op jit(solution)/shard_map/gather | solution.py:188
  336.6 13.9 %scatter_custom_fusion.2 = f32[28,3072]{0,1:T(8,128)S(1)} fusion(s32[2048]{0:T(1024)} %bitcast.413, f32[2048,28]{1,0:T(8,128)} %bitcast.373, f32[]{:T(128)} %constant.38.clone.1), kind=kCustom, calls=%fused_computation.57 | custom fusion | flops 57344 | bytes 344576 | tf_op jit(solution)/shard_map/scatter-add | solution.py:219
  363.1 17.9 %scatter_custom_fusion.4 = f32[28,5120]{0,1:T(8,128)S(1)} fusion(s32[3072]{0:T(1024)} %bitcast.404, f32[3072,28]{1,0:T(8,128)} %copy.366, f32[]{:T(128)} %constant.38.clone.1), kind=kCustom, calls=%fused_computation.34 | custom fusion | flops 86016 | bytes 573952 | tf_op jit(solution)/shard_map/transpose(jvp())/scatter-add | solution.py:68
  448.8 13.6 %scatter_custom_fusion.6 = f32[28,3072]{0,1:T(8,128)S(1)} fusion(s32[2048]{0:T(1024)} %bitcast.414, f32[2048,28]{1,0:T(8,128)S(1)} %bitcast.374, f32[]{:T(128)} %constant.38.clone.1), kind=kCustom, calls=%fused_computation.55 | custom fusion | flops 57344 | bytes 344576 | tf_op jit(solution)/shard_map/scatter-add | solution.py:219
  474.9 17.9 %scatter_custom_fusion.8 = f32[28,5120]{0,1:T(8,128)S(1)} fusion(s32[3072]{0:T(1024)} %bitcast.405, f32[3072,28]{1,0:T(8,128)} %copy.395, f32[]{:T(128)} %constant.38.clone.1), kind=kCustom, calls=%fused_computation.32 | custom fusion | flops 86016 | bytes 573952 | tf_op jit(solution)/shard_map/transpose(jvp())/scatter-add | solution.py:68
  515.0 36.4 %all-gather.5 = f32[128,2,512]{2,1,0:T(2,128)S(1)} all-gather(f32[1,2,512]{2,1,0:T(2,128)S(1)} %copy.420), channel_id=4, replica_groups=mesh['gx'=16,'gy'=8] {'gx','gy'}, dimensions={0}, use_global_device_ids=true | all-gather | bytes 528384 | tf_op jit(solution)/shard_map/all_gather | solution.py:240
  554.3 33.9 %all-gather.4 = f32[128,2,512]{2,1,0:T(2,128)S(1)} all-gather(f32[1,2,512]{2,1,0:T(2,128)S(1)} %copy.415), channel_id=3, replica_groups=mesh['gx'=16,'gy'=8] {'gx','gy'}, dimensions={0}, use_global_device_ids=true | all-gather | bytes 528384 | tf_op jit(solution)/shard_map/all_gather | solution.py:240
  590.3 34.0 %all-gather.3 = f32[128,2,512]{2,1,0:T(2,128)S(1)} all-gather(f32[1,2,512]{2,1,0:T(2,128)S(1)} %copy.410), channel_id=2, replica_groups=mesh['gx'=16,'gy'=8] {'gx','gy'}, dimensions={0}, use_global_device_ids=true | all-gather | bytes 528384 | tf_op jit(solution)/shard_map/all_gather | solution.py:240
  661.5 13.6 %scatter_custom_fusion.10 = f32[28,3072]{0,1:T(8,128)S(1)} fusion(s32[2048]{0:T(1024)} %bitcast.415, f32[2048,28]{1,0:T(8,128)S(1)} %bitcast.372, f32[]{:T(128)} %constant.38.clone.1), kind=kCustom, calls=%fused_computation.53 | custom fusion | flops 57344 | bytes 344576 | tf_op jit(solution)/shard_map/scatter-add | solution.py:219
  (745 shorter events, 368.1 us)
Async XLA Ops:
  40.8 41.3 %collective-permute-start = (bf16[1,28,256]{2,1,0:T(8,128)(2,1)}, bf16[1,28,256]{2,1,0:T(8,128)(2,1)}, u32[]{:S(2)}, u32[]{:S(2)}) collective-permute-start(bf16[1,28,256]{2,1,0:T(8,128)(2,1)} %get-tuple-element.112), channel_id=1, source_target_pairs={{0,8},{8,16},{16,24},{24,32},{32,40},{40,48},{48,56},{56,64},{64,7... | collective-permute-start | bytes 43016 | tf_op jit(solution)/shard_map/ppermute | solution.py:20
  43.9 42.8 %collective-permute-start.2 = (bf16[1,28,256]{2,1,0:T(8,128)(2,1)}, bf16[1,28,256]{2,1,0:T(8,128)(2,1)}, u32[]{:S(2)}, u32[]{:S(2)}) collective-permute-start(bf16[1,28,256]{2,1,0:T(8,128)(2,1)} %get-tuple-element.111), channel_id=1, source_target_pairs={{0,8},{8,16},{16,24},{24,32},{32,40},{40,48},{48,56},{56,64},{64,7... | collective-permute-start | bytes 43016 | tf_op jit(solution)/shard_map/ppermute | solution.py:20
  47.0 42.4 %collective-permute-start.3 = (bf16[1,28,256]{2,1,0:T(8,128)(2,1)}, bf16[1,28,256]{2,1,0:T(8,128)(2,1)}, u32[]{:S(2)}, u32[]{:S(2)}) collective-permute-start(bf16[1,28,256]{2,1,0:T(8,128)(2,1)} %get-tuple-element.110), channel_id=1, source_target_pairs={{0,8},{8,16},{16,24},{24,32},{32,40},{40,48},{48,56},{56,64},{64,7... | collective-permute-start | bytes 43016 | tf_op jit(solution)/shard_map/ppermute | solution.py:20
  49.9 41.8 %collective-permute-start.5 = (bf16[1,28,256]{2,1,0:T(8,128)(2,1)}, bf16[1,28,256]{2,1,0:T(8,128)(2,1)}, u32[]{:S(2)}, u32[]{:S(2)}) collective-permute-start(bf16[1,28,256]{2,1,0:T(8,128)(2,1)} %get-tuple-element.109), channel_id=1, source_target_pairs={{0,1},{1,2},{2,3},{3,4},{4,5},{5,6},{6,7},{8,9},{9,10},{10,11},{11... | collective-permute-start | bytes 43016 | tf_op jit(solution)/shard_map/ppermute | solution.py:20
  54.5 40.3 %collective-permute-start.6 = (bf16[1,28,256]{2,1,0:T(8,128)(2,1)}, bf16[1,28,256]{2,1,0:T(8,128)(2,1)}, u32[]{:S(2)}, u32[]{:S(2)}) collective-permute-start(bf16[1,28,256]{2,1,0:T(8,128)(2,1)} %get-tuple-element.108), channel_id=1, source_target_pairs={{1,0},{2,1},{3,2},{4,3},{5,4},{6,5},{7,6},{9,8},{10,9},{11,10},{12... | collective-permute-start | bytes 43016 | tf_op jit(solution)/shard_map/ppermute | solution.py:20
  124.0 36.8 %collective-permute-start.24 = (bf16[1,28,256]{2,1,0:T(8,128)(2,1)S(1)}, bf16[1,28,256]{2,1,0:T(8,128)(2,1)}, u32[]{:S(2)}, u32[]{:S(2)}) collective-permute-start(bf16[1,28,256]{2,1,0:T(8,128)(2,1)S(1)} %get-tuple-element.104), channel_id=1, source_target_pairs={{0,8},{8,16},{16,24},{24,32},{32,40},{40,48},{48,56},{56,64},{64,7... | collective-permute-start | bytes 43016 | tf_op jit(solution)/shard_map/ppermute | solution.py:20
  125.9 36.8 %collective-permute-start.27 = (bf16[1,28,256]{2,1,0:T(8,128)(2,1)S(1)}, bf16[1,28,256]{2,1,0:T(8,128)(2,1)}, u32[]{:S(2)}, u32[]{:S(2)}) collective-permute-start(bf16[1,28,256]{2,1,0:T(8,128)(2,1)S(1)} %get-tuple-element.102), channel_id=1, source_target_pairs={{0,8},{8,16},{16,24},{24,32},{32,40},{40,48},{48,56},{56,64},{64,7... | collective-permute-start | bytes 43016 | tf_op jit(solution)/shard_map/ppermute | solution.py:20
  150.4 59.4 %collective-permute-start.31 = (bf16[1,28,256]{2,1,0:T(8,128)(2,1)}, bf16[1,28,256]{2,1,0:T(8,128)(2,1)}, u32[]{:S(2)}, u32[]{:S(2)}) collective-permute-start(bf16[1,28,256]{2,1,0:T(8,128)(2,1)} %get-tuple-element.99), channel_id=1, source_target_pairs={{8,0},{16,8},{24,16},{32,24},{40,32},{48,40},{56,48},{64,56},{72,6... | collective-permute-start | bytes 43016 | tf_op jit(solution)/shard_map/ppermute | solution.py:20
  156.7 55.2 %collective-permute-start.34 = (bf16[1,28,256]{2,1,0:T(8,128)(2,1)}, bf16[1,28,256]{2,1,0:T(8,128)(2,1)}, u32[]{:S(2)}, u32[]{:S(2)}) collective-permute-start(bf16[1,28,256]{2,1,0:T(8,128)(2,1)} %get-tuple-element.97), channel_id=1, source_target_pairs={{8,0},{16,8},{24,16},{32,24},{40,32},{48,40},{56,48},{64,56},{72,6... | collective-permute-start | bytes 43016 | tf_op jit(solution)/shard_map/ppermute | solution.py:20
  160.8 56.6 %collective-permute-start.48 = (bf16[1,28,256]{2,1,0:T(8,128)(2,1)}, bf16[1,28,256]{2,1,0:T(8,128)(2,1)}, u32[]{:S(2)}, u32[]{:S(2)}) collective-permute-start(bf16[1,28,256]{2,1,0:T(8,128)(2,1)} %get-tuple-element.96), channel_id=1, source_target_pairs={{0,8},{8,16},{16,24},{24,32},{32,40},{40,48},{48,56},{56,64},{64,7... | collective-permute-start | bytes 43016 | tf_op jit(solution)/shard_map/ppermute | solution.py:20
  162.7 58.0 %collective-permute-start.25 = (bf16[1,28,256]{2,1,0:T(8,128)(2,1)}, bf16[1,28,256]{2,1,0:T(8,128)(2,1)}, u32[]{:S(2)}, u32[]{:S(2)}) collective-permute-start(bf16[1,28,256]{2,1,0:T(8,128)(2,1)} %collective-permute-done.24), channel_id=1, source_target_pairs={{0,1},{1,2},{2,3},{3,4},{4,5},{5,6},{6,7},{8,9},{9,10},{10,11},{11... | collective-permute-start | bytes 43016 | tf_op jit(solution)/shard_map/ppermute | solution.py:20
  167.2 58.0 %collective-permute-start.28 = (bf16[1,28,256]{2,1,0:T(8,128)(2,1)}, bf16[1,28,256]{2,1,0:T(8,128)(2,1)}, u32[]{:S(2)}, u32[]{:S(2)}) collective-permute-start(bf16[1,28,256]{2,1,0:T(8,128)(2,1)} %collective-permute-done.27), channel_id=1, source_target_pairs={{1,0},{2,1},{3,2},{4,3},{5,4},{6,5},{7,6},{9,8},{10,9},{11,10},{12... | collective-permute-start | bytes 43016 | tf_op jit(solution)/shard_map/ppermute | solution.py:20
  237.8 35.4 %collective-permute-start.56 = (bf16[1,28,256]{2,1,0:T(8,128)(2,1)}, bf16[1,28,256]{2,1,0:T(8,128)(2,1)}, u32[]{:S(2)}, u32[]{:S(2)}) collective-permute-start(bf16[1,28,256]{2,1,0:T(8,128)(2,1)} %collective-permute-done.55), channel_id=1, source_target_pairs={{0,1},{1,2},{2,3},{3,4},{4,5},{5,6},{6,7},{8,9},{9,10},{10,11},{11... | collective-permute-start | bytes 43016 | tf_op jit(solution)/shard_map/ppermute | solution.py:20
  241.5 37.0 %collective-permute-start.59 = (bf16[1,28,256]{2,1,0:T(8,128)(2,1)}, bf16[1,28,256]{2,1,0:T(8,128)(2,1)}, u32[]{:S(2)}, u32[]{:S(2)}) collective-permute-start(bf16[1,28,256]{2,1,0:T(8,128)(2,1)} %collective-permute-done.58), channel_id=1, source_target_pairs={{1,0},{2,1},{3,2},{4,3},{5,4},{6,5},{7,6},{9,8},{10,9},{11,10},{12... | collective-permute-start | bytes 43016 | tf_op jit(solution)/shard_map/ppermute | solution.py:20
  243.4 55.2 %collective-permute-start.12 = (f32[28,256]{1,0:T(8,128)}, f32[28,256]{1,0:T(8,128)}, u32[]{:S(2)}, u32[]{:S(2)}) collective-permute-start(f32[28,256]{1,0:T(8,128)} %bitcast.43), channel_id=1, source_target_pairs={{0,8},{8,16},{16,24},{24,32},{32,40},{40,48},{48,56},{56,64},{64,7... | collective-permute-start | bytes 86024 | tf_op jit(solution)/shard_map/ppermute | solution.py:20
  266.9 35.9 %collective-permute-start.14 = (f32[28,256]{1,0:T(8,128)}, f32[28,256]{1,0:T(8,128)}, u32[]{:S(2)}, u32[]{:S(2)}) collective-permute-start(f32[28,256]{1,0:T(8,128)} %bitcast.44), channel_id=1, source_target_pairs={{0,8},{8,16},{16,24},{24,32},{32,40},{40,48},{48,56},{56,64},{64,7... | collective-permute-start | bytes 86024 | tf_op jit(solution)/shard_map/ppermute | solution.py:20
  269.5 37.7 %collective-permute-start.15 = (f32[28,256]{1,0:T(8,128)}, f32[28,256]{1,0:T(8,128)}, u32[]{:S(2)}, u32[]{:S(2)}) collective-permute-start(f32[28,256]{1,0:T(8,128)} %bitcast.45), channel_id=1, source_target_pairs={{0,8},{8,16},{16,24},{24,32},{32,40},{40,48},{48,56},{56,64},{64,7... | collective-permute-start | bytes 86024 | tf_op jit(solution)/shard_map/ppermute | solution.py:20
  273.2 37.3 %collective-permute-start.17 = (f32[28,256]{1,0:T(8,128)}, f32[28,256]{1,0:T(8,128)}, u32[]{:S(2)}, u32[]{:S(2)}) collective-permute-start(f32[28,256]{1,0:T(8,128)} %bitcast.46), channel_id=1, source_target_pairs={{0,1},{1,2},{2,3},{3,4},{4,5},{5,6},{6,7},{8,9},{9,10},{10,11},{11... | collective-permute-start | bytes 86024 | tf_op jit(solution)/shard_map/ppermute | solution.py:20
  278.5 36.6 %collective-permute-start.18 = (f32[28,256]{1,0:T(8,128)}, f32[28,256]{1,0:T(8,128)}, u32[]{:S(2)}, u32[]{:S(2)}) collective-permute-start(f32[28,256]{1,0:T(8,128)} %bitcast.47), channel_id=1, source_target_pairs={{1,0},{2,1},{3,2},{4,3},{5,4},{6,5},{7,6},{9,8},{10,9},{11,10},{12... | collective-permute-start | bytes 86024 | tf_op jit(solution)/shard_map/ppermute | solution.py:20
  495.7 134.1 %collective-permute-start.60 = (f32[28,256]{1,0:T(8,128)}, f32[28,256]{1,0:T(8,128)}, u32[]{:S(2)}, u32[]{:S(2)}) collective-permute-start(f32[28,256]{1,0:T(8,128)} %bitcast.119), channel_id=1, source_target_pairs={{0,8},{8,16},{16,24},{24,32},{32,40},{40,48},{48,56},{56,64},{64,7... | collective-permute-start | bytes 86024 | tf_op jit(solution)/shard_map/ppermute | solution.py:20
  499.3 134.9 %collective-permute-start.62 = (f32[28,256]{1,0:T(8,128)}, f32[28,256]{1,0:T(8,128)}, u32[]{:S(2)}, u32[]{:S(2)}) collective-permute-start(f32[28,256]{1,0:T(8,128)} %bitcast.120), channel_id=1, source_target_pairs={{0,8},{8,16},{16,24},{24,32},{32,40},{40,48},{48,56},{56,64},{64,7... | collective-permute-start | bytes 86024 | tf_op jit(solution)/shard_map/ppermute | solution.py:20
  502.8 135.7 %collective-permute-start.63 = (f32[28,256]{1,0:T(8,128)}, f32[28,256]{1,0:T(8,128)}, u32[]{:S(2)}, u32[]{:S(2)}) collective-permute-start(f32[28,256]{1,0:T(8,128)} %bitcast.121), channel_id=1, source_target_pairs={{0,8},{8,16},{16,24},{24,32},{32,40},{40,48},{48,56},{56,64},{64,7... | collective-permute-start | bytes 86024 | tf_op jit(solution)/shard_map/ppermute | solution.py:20
  506.3 134.9 %collective-permute-start.65 = (f32[28,256]{1,0:T(8,128)}, f32[28,256]{1,0:T(8,128)}, u32[]{:S(2)}, u32[]{:S(2)}) collective-permute-start(f32[28,256]{1,0:T(8,128)} %bitcast.122), channel_id=1, source_target_pairs={{0,1},{1,2},{2,3},{3,4},{4,5},{5,6},{6,7},{8,9},{9,10},{10,11},{11... | collective-permute-start | bytes 86024 | tf_op jit(solution)/shard_map/ppermute | solution.py:20
  510.8 133.6 %collective-permute-start.66 = (f32[28,256]{1,0:T(8,128)S(1)}, f32[28,256]{1,0:T(8,128)}, u32[]{:S(2)}, u32[]{:S(2)}) collective-permute-start(f32[28,256]{1,0:T(8,128)S(1)} %bitcast.408), channel_id=1, source_target_pairs={{1,0},{2,1},{3,2},{4,3},{5,4},{6,5},{7,6},{9,8},{10,9},{11,10},{12... | collective-permute-start | bytes 86024 | tf_op jit(solution)/shard_map/ppermute | solution.py:20
  (202 other events, 3131.9 us)
